TPU v7x, 32 devices: a whole 2x2x4 slice. The times are simulated.
32 devices in a mesh: mem: 16 (over z, y, core), lat: 2 (over x).
Axes of the slice: x: 2, y: 2, z: 4, core: 2. Of those that a mesh axis runs over, the one named last changes fastest.
Arguments:
- controls: bfloat16 [64, 64, 256, 256], P('mem', None, 'lat'), may hold values from -6 to 6
- spread: bfloat16 [64, 64, 256, 256], P('mem', None, 'lat'), may hold values from -1.5 to 1.5
- classes: int32 [256, 256], P('lat'), may hold values from 0 to 7
- prec_table: float32 [8, 64], replicated, may hold values from 0.25 to 4
- vert_loc: bfloat16 [64, 64], replicated, may hold values from 0 to 1
- lon_loc: bfloat16 [256, 256], replicated, may hold values from 0 to 1
- lat_loc: bfloat16 [256, 256], replicated, may hold values from 0 to 1
Outputs:
- localized: bfloat16 [64, 64, 256, 256], P('mem', None, 'lat')
All inputs are finite; a program needn't handle non-finite values.
Results may differ from a plain program's by a relative error of at most 0.0064.
Values may be sent and summed in bfloat16 or wider, within the bound.
A program may use at most 128 MiB of HBM per device.

v0:
```python
import jax
import jax.numpy as jnp
from jax import lax
from jax.sharding import PartitionSpec as P


def lookup(table, classes):
    numbers = jnp.arange(table.shape[0], dtype=jnp.int32)
    onehot = (classes[None, :, :] == numbers[:, None, None]).astype(jnp.float32)
    return jnp.einsum("kl,kab->lab", table, onehot, precision=lax.Precision.HIGHEST)


def local(controls, spread, classes, prec_table, vert_loc, lon_loc, lat_loc):
    partial_value = jnp.sum(spread.astype(jnp.float32) * controls.astype(jnp.float32), axis=0)
    shares = lax.psum_scatter(partial_value, "mem", scatter_dimension=0, tiled=True)
    level_count = shares.shape[0]
    table_rows = lax.dynamic_slice_in_dim(
        prec_table, lax.axis_index("mem") * level_count, level_count, 1
    )
    weighted_part = shares * lookup(table_rows, classes)
    weighted = lax.all_gather(weighted_part, "mem", axis=0, tiled=True)
    adjoint = (spread.astype(jnp.float32) * weighted[None]).astype(jnp.bfloat16)
    along_lon = jnp.einsum(
        "mlac,bc->mlab", adjoint, lon_loc, preferred_element_type=jnp.float32
    ).astype(jnp.bfloat16)
    sending = jnp.einsum(
        "lj,mjab->mlab", vert_loc, along_lon, preferred_element_type=jnp.float32
    ).astype(jnp.bfloat16)
    return jnp.einsum(
        "ac,mlcb->mlba",
        lat_loc,
        lax.all_to_all(sending, "lat", split_axis=3, concat_axis=2, tiled=True),
        preferred_element_type=jnp.float32,
    ).astype(jnp.bfloat16)


def solution(mesh):
    return jax.shard_map(
        local,
        mesh=mesh,
        in_specs=(
            P("mem", None, "lat", None),
            P("mem", None, "lat", None),
            P("lat", None),
            P(),
            P(),
            P(),
            P(),
        ),
        out_specs=P("mem", None, "lat", None),
        check_vma=False,
    )
```

profile of v0, /device:TPU:0, one launch (start us, length us, event | category | flops | bytes accessed | tf_op | source)
XLA Modules:
  0.0 539.2 jit_solution(17640405347638670509)
XLA Ops:
  6.5 0.0 copy-start
  6.5 0.0 copy-start.5
  6.5 0.0 copy-start.3
  6.5 0.0 reduce-scatter.2.cloned.1.call-start
  6.5 17.7 %fusion = f32[64,128,256]{2,1,0:T(8,128)} fusion(bf16[4,64,128,256]{3,2,1,0:T(8,128)(2,1)} %param.8, bf16[4,64,128,256]{3,2,1,0:T(8,128)(2,1)} %param.7), kind=kLoop, calls=%fused_computation.2 | loop fusion | flops 31457280 | bytes 41943040 | tf_op jit(solution)/shard_map/reduce_sum | solution.py:14
  24.3 0.0 reduce-scatter.2.cloned.1.call-update
  24.3 0.0 all-gather.2.cloned.1.call-start
  24.3 0.0 copy-done.5
  24.3 0.0 copy-done.3
  24.4 0.7 fusion.14
  25.1 105.5 %reduce-scatter.2.cloned.1.call-done = f32[4,128,256]{2,1,0:T(8,128)} async-done(((f32[64,128,256]{2,1,0:T(8,128)}), f32[4,128,256]{2,1,0:T(8,128)}) %reduce-scatter.2.cloned.1.call-update) | async-done | bytes 524304 | tf_op jit(solution)/shard_map/reduce_scatter | solution.py:15
  130.6 2.0 copy_multiply_fusion
  132.6 0.0 all-gather.2.cloned.1.call-update
  132.6 0.0 copy-start.4
  132.6 74.1 %all-gather.2.cloned.1.call-done = f32[64,128,256]{2,1,0:T(8,128)} async-done(((f32[4,128,256]{2,1,0:T(8,128)}), f32[64,128,256]{2,1,0:T(8,128)}) %all-gather.2.cloned.1.call-update) | async-done | bytes 8388624 | tf_op jit(solution)/shard_map/all_gather | solution.py:21
  206.7 16.6 %fusion.1 = bf16[4,64,128,256]{3,2,1,0:T(8,128)(2,1)} fusion(bf16[4,64,128,256]{3,2,1,0:T(8,128)(2,1)} %param.8, f32[64,128,256]{2,1,0:T(8,128)} %all-gather.2.cloned.1.call-done), kind=kLoop, calls=%fused_computation.3 | loop fusion | flops 25165824 | bytes 41943040 | tf_op jit(solution)/shard_map/convert_element_type | solution.py:22
  223.4 0.0 copy-done
  223.4 0.0 copy-done.4
  223.4 19.1 %convert_bitcast_fusion = bf16[4,64,128,256]{3,1,2,0:T(8,128)(2,1)} fusion(bf16[4,64,128,256]{3,2,1,0:T(8,128)(2,1)} %fusion.1, bf16[256,256]{1,0:T(8,128)(2,1)S(1)} %copy-done, bf16[64,64]{1,0:T(8,128)(2,1)S(1)} %copy-done.4), kind=kOutput, calls=%fused_computation.7 | convolution fusion | flops 5385486336 | bytes 33693696 | tf_op jit(solution)/shard_map/lj,mjab->mlab/dot_general | solution.py:26
  242.5 25.8 %copy.25 = bf16[4,64,128,256]{2,1,0,3:T(8,128)(2,1)} copy(bf16[4,64,128,256]{3,1,2,0:T(8,128)(2,1)} %convert_bitcast_fusion) | data formatting | bytes 33554432 | tf_op jit(solution)/shard_map/convert_element_type | solution.py:28
  268.3 188.7 %all_to_all.18 = bf16[4,64,128,256]{2,1,0,3:T(8,128)(2,1)S(1)} all-to-all(bf16[4,64,128,256]{2,1,0,3:T(8,128)(2,1)} %copy.25), channel_id=1, replica_groups=mesh['mem'=16,'lat'=2] {'lat'}, dimensions={3} | all-to-all | bytes 33554432 | tf_op jit(solution)/shard_map/all_to_all | solution.py:32
  457.0 36.5 %copy.41 = bf16[4,64,128,2,128]{2,3,4,1,0:T(2,128)(2,1)} copy(bf16[4,64,128,2,128]{2,1,0,4,3:T(8,128)(2,1)S(1)} %bitcast.29) | data formatting | bytes 33554432 | tf_op jit(solution)/shard_map/all_to_all | solution.py:32
  493.5 0.0 copy-start.2
  493.5 0.0 copy-start.1
  493.5 27.0 %all_to_all.16 = bf16[4,64,256,128]{2,3,1,0:T(8,128)(2,1)} reshape(bf16[4,64,2,128,128]{3,2,4,1,0:T(2,128)(2,1)} %bitcast.30) | data formatting | bytes 33554432 | tf_op jit(solution)/shard_map/all_to_all | solution.py:32
  520.4 0.0 copy-done.2
  520.4 11.9 %convolution_convert_fusion = bf16[4,64,128,256]{3,2,1,0:T(8,128)(2,1)} fusion(bf16[4,64,256,128]{2,3,1,0:T(8,128)(2,1)} %all_to_all.16, bf16[256,256]{1,0:T(8,128)(2,1)S(1)} %copy-done.2), kind=kOutput, calls=%fused_computation.10 | convolution fusion | flops 4303355904 | bytes 33685504 | tf_op jit(solution)/shard_map/ac,mlcb->mlba/dot_general | solution.py:29
  532.4 0.0 copy-done.1
Async XLA Ops:
  6.5 216.8 %copy-start = (bf16[256,256]{1,0:T(8,128)(2,1)S(1)}, bf16[256,256]{1,0:T(8,128)(2,1)}, u32[]{:S(2)}) copy-start(bf16[256,256]{1,0:T(8,128)(2,1)} %param.12) | copy-start | bytes 393220
  6.5 17.8 %copy-start.5 = (f32[8,64]{1,0:T(8,128)S(1)}, f32[8,64]{1,0:T(8,128)}, u32[]{:S(2)}) copy-start(f32[8,64]{1,0:T(8,128)} %param.10) | copy-start | bytes 6148
  6.5 17.8 %copy-start.3 = (s32[128,256]{1,0:T(8,128)S(1)}, s32[128,256]{1,0:T(8,128)}, u32[]{:S(2)}) copy-start(s32[128,256]{1,0:T(8,128)} %param.9) | copy-start | bytes 393220
  6.5 124.1 %reduce-scatter.2.cloned.1.call-start = ((), (), s32[]{:S(2)}) async-start(), calls=%async_computation.2 | async-start | bytes 8912896 | tf_op jit(solution)/shard_map/reduce_scatter | solution.py:15
  24.3 182.5 %all-gather.2.cloned.1.call-start = ((), (), s32[]{:S(2)}) async-start(), calls=%async_computation.3 | async-start | bytes 8912896 | tf_op jit(solution)/shard_map/all_gather | solution.py:21
  132.6 90.8 %copy-start.4 = (bf16[64,64]{1,0:T(8,128)(2,1)S(1)}, bf16[64,64]{1,0:T(8,128)(2,1)}, u32[]{:S(2)}) copy-start(bf16[64,64]{1,0:T(8,128)(2,1)} %param.11) | copy-start | bytes 24580
  493.5 27.0 %copy-start.2 = (bf16[256,256]{1,0:T(8,128)(2,1)S(1)}, bf16[256,256]{1,0:T(8,128)(2,1)}, u32[]{:S(2)}) copy-start(bf16[256,256]{1,0:T(8,128)(2,1)} %param.13) | copy-start | bytes 393220
  493.5 38.9 %copy-start.1 = (bf16[256,256]{1,0:T(8,128)(2,1)S(1)}, bf16[256,256]{1,0:T(8,128)(2,1)}, u32[]{:S(2)}) copy-start(bf16[256,256]{1,0:T(8,128)(2,1)} %param.12) | copy-start | bytes 393220
Sparse Core Ops, SparseCore 0:
  24.4 106.1 reduce-scatter.1
  132.8 73.9 all-gather.1
where the time goes:
time: 541 us; the launch traced here: 539 us
  blocking collectives  189 us (35%)
  waiting for transfers between devices  180 us (33%)
  local copies, waits for them, and re-layouts  89.2 us (16%)
  other arithmetic  36.3 us (7%)
  matrix products  31.8 us (6%)
  between operations  13.4 us (2%)
    all_to_all x1, blocking collectives, local(): lax.all_to_all(sending, 'lat', split_axis=3, concat_axis=2, tiled=True)  189 us
    reduce_scatter x1, waiting for transfers between devices, local(): lax.psum_scatter(partial_value, 'mem', scatter_dimension=0, tiled=True)  106 us
    all_gather x1, waiting for transfers between devices, local(): weighted = lax.all_gather(weighted_part, 'mem', axis=0, tiled=True)  74.1 us
    all_to_all x2, local copies, waits for them, and re-layouts, local(): lax.all_to_all(sending, 'lat', split_axis=3, concat_axis=2, tiled=True)  63.4 us
    convert_element_type x1, local copies, waits for them, and re-layouts, local(): sending = jnp.einsum('lj,mjab->mlab', vert_loc, along_lon, preferred_elem...  25.8 us
    dot_general x1, matrix products, local(): jnp.einsum('lj,mjab->mlab', vert_loc, along_lon, preferred_element_type=j...  19.1 us
    reduce_sum x1, other arithmetic, local(): jnp.sum(spread.astype(jnp.float32) * controls.astype(jnp.float32), axis=0)  17.7 us
    convert_element_type x1, other arithmetic, local(): adjoint = (spread.astype(jnp.float32) * weighted[None]).astype(jnp.bfloat16)  16.6 us
  transfers between devices with their start and end apart: 2, of which 2 were waited for; matrix products, arithmetic and copies ran while one was open for 0% of the time, Pallas kernels for 0%

commit v1 on v0

--- a/solution.py
+++ b/solution.py
@@ -29,7 +29,12 @@
     return jnp.einsum(
         "ac,mlcb->mlba",
         lat_loc,
-        lax.all_to_all(sending, "lat", split_axis=3, concat_axis=2, tiled=True),
+        jnp.concatenate(
+            lax.all_to_all(
+                jnp.stack(jnp.split(sending, lax.axis_size("lat"), axis=3)), "lat", 0, 0
+            ),
+            axis=2,
+        ),
         preferred_element_type=jnp.float32,
     ).astype(jnp.bfloat16)
 

time: 541 us -> 502 us (0.928)
  local copies, waits for them, and re-layouts: 89.2 us -> 47.5 us
  other arithmetic: 36.3 us -> 42.5 us
    all_to_all x2 -> x0, local copies, waits for them, and re-layouts: 63.4 us -> none  [local(): lax.all_to_all(sending, 'lat', split_axis=3, concat_axis=2, tiled=True)]
    reshape x0 -> x1, local copies, waits for them, and re-layouts: none -> 36.9 us  [local(): jnp.concatenate(lax.all_to_all(jnp.stack(jnp.split(sending, lax.axis_size...]
    convert_element_type x1 -> x0, local copies, waits for them, and re-layouts: 25.8 us -> none  [local(): sending = jnp.einsum('lj,mjab->mlab', vert_loc, along_lon, preferred_elem...]
    another operation x0 -> x1, local copies, waits for them, and re-layouts: none -> 10.7 us  [local(): jnp.stack(jnp.split(sending, lax.axis_size('lat'), axis=3))]
    another operation x0 -> x1, other arithmetic: none -> 6.25 us  [local(): jnp.stack(jnp.split(sending, lax.axis_size('lat'), axis=3))]
where the time goes in v1:
time: 502 us
  blocking collectives  187 us (37%)
  waiting for transfers between devices  180 us (36%)
  local copies, waits for them, and re-layouts  47.5 us (9%)
  other arithmetic  42.5 us (8%)
  matrix products  31.8 us (6%)
  between operations  13.5 us (3%)
    all_to_all x1, blocking collectives, local(): lax.all_to_all(jnp.stack(jnp.split(sending, lax.axis_size('lat'), axis=3)...  187 us
    reduce_scatter x1, waiting for transfers between devices, local(): lax.psum_scatter(partial_value, 'mem', scatter_dimension=0, tiled=True)  106 us
    all_gather x1, waiting for transfers between devices, local(): weighted = lax.all_gather(weighted_part, 'mem', axis=0, tiled=True)  74.1 us
    reshape x1, local copies, waits for them, and re-layouts, local(): jnp.concatenate(lax.all_to_all(jnp.stack(jnp.split(sending, lax.axis_size...  36.9 us
    dot_general x1, matrix products, local(): jnp.einsum('lj,mjab->mlab', vert_loc, along_lon, preferred_element_type=j...  19.1 us
    reduce_sum x1, other arithmetic, local(): jnp.sum(spread.astype(jnp.float32) * controls.astype(jnp.float32), axis=0)  17.7 us
    convert_element_type x1, other arithmetic, local(): adjoint = (spread.astype(jnp.float32) * weighted[None]).astype(jnp.bfloat16)  16.6 us
    dot_general x1, matrix products, local(): jnp.einsum('ac,mlcb->mlba', lat_loc, jnp.concatenate(lax.all_to_all(jnp.s...  12 us
  transfers between devices with their start and end apart: 2, of which 2 were waited for; matrix products, arithmetic and copies ran while one was open for 0% of the time, Pallas kernels for 0%

profile of v1, /device:TPU:0, one launch (start us, length us, event | category | flops | bytes accessed | tf_op | source)
XLA Modules:
  0.0 501.8 jit_solution(6047835043654997496)
XLA Ops:
  6.5 0.0 copy-start
  6.5 0.0 copy-start.5
  6.5 0.0 copy-start.3
  6.5 0.0 reduce-scatter.2.cloned.1.call-start
  6.5 17.7 %fusion = f32[64,128,256]{2,1,0:T(8,128)} fusion(bf16[4,64,128,256]{3,2,1,0:T(8,128)(2,1)} %param.8, bf16[4,64,128,256]{3,2,1,0:T(8,128)(2,1)} %param.7), kind=kLoop, calls=%fused_computation.2 | loop fusion | flops 31457280 | bytes 41943040 | tf_op jit(solution)/shard_map/reduce_sum | solution.py:14
  24.3 0.0 reduce-scatter.2.cloned.1.call-update
  24.3 0.0 all-gather.2.cloned.1.call-start
  24.3 0.0 copy-done.5
  24.3 0.0 copy-done.3
  24.4 0.7 fusion.14
  25.1 105.5 %reduce-scatter.2.cloned.1.call-done = f32[4,128,256]{2,1,0:T(8,128)} async-done(((f32[64,128,256]{2,1,0:T(8,128)}), f32[4,128,256]{2,1,0:T(8,128)}) %reduce-scatter.2.cloned.1.call-update) | async-done | bytes 524304 | tf_op jit(solution)/shard_map/reduce_scatter | solution.py:15
  130.6 2.0 copy_multiply_fusion
  132.6 0.0 all-gather.2.cloned.1.call-update
  132.6 0.0 copy-start.4
  132.6 74.1 %all-gather.2.cloned.1.call-done = f32[64,128,256]{2,1,0:T(8,128)} async-done(((f32[4,128,256]{2,1,0:T(8,128)}), f32[64,128,256]{2,1,0:T(8,128)}) %all-gather.2.cloned.1.call-update) | async-done | bytes 8388624 | tf_op jit(solution)/shard_map/all_gather | solution.py:21
  206.7 16.6 %fusion.1 = bf16[4,64,128,256]{3,2,1,0:T(8,128)(2,1)} fusion(bf16[4,64,128,256]{3,2,1,0:T(8,128)(2,1)} %param.8, f32[64,128,256]{2,1,0:T(8,128)} %all-gather.2.cloned.1.call-done), kind=kLoop, calls=%fused_computation.3 | loop fusion | flops 25165824 | bytes 41943040 | tf_op jit(solution)/shard_map/convert_element_type | solution.py:22
  223.4 0.0 copy-done
  223.4 0.0 copy-done.4
  223.4 19.1 %convert_bitcast_fusion = bf16[4,64,128,256]{3,1,2,0:T(8,128)(2,1)} fusion(bf16[4,64,128,256]{3,2,1,0:T(8,128)(2,1)} %fusion.1, bf16[256,256]{1,0:T(8,128)(2,1)S(1)} %copy-done, bf16[64,64]{1,0:T(8,128)(2,1)S(1)} %copy-done.4), kind=kOutput, calls=%fused_computation.7 | convolution fusion | flops 5385486336 | bytes 33693696 | tf_op jit(solution)/shard_map/lj,mjab->mlab/dot_general | solution.py:26
  242.5 10.7 %slice_bitcast_fusion.1 = (bf16[1,4,64,128,128]{4,2,3,1,0:T(8,128)(2,1)S(1)}, bf16[1,4,64,128,128]{4,2,3,1,0:T(8,128)(2,1)}) fusion(bf16[4,64,128,256]{3,1,2,0:T(8,128)(2,1)} %convert_bitcast_fusion), kind=kLoop, calls=%fused_computation.12 | loop fusion | bytes 33554432 | tf_op jit(solution)/shard_map/stack | solution.py:34
  253.2 6.2 %pad_maximum_fusion = bf16[2,4,64,128,128]{4,2,3,1,0:T(8,128)(2,1)S(1)} fusion(bf16[1,4,64,128,128]{4,2,3,1,0:T(8,128)(2,1)} %get-tuple-element.6, bf16[1,4,64,128,128]{4,2,3,1,0:T(8,128)(2,1)S(1)} %get-tuple-element.5), kind=kLoop, calls=%fused_computation.4 | loop fusion | flops 8388608 | bytes 33554432 | tf_op jit(solution)/shard_map/stack | solution.py:34
  259.4 186.7 %all_to_all.5 = bf16[2,4,64,128,128]{4,2,3,1,0:T(8,128)(2,1)S(1)} all-to-all(bf16[2,4,64,128,128]{4,2,3,1,0:T(8,128)(2,1)S(1)} %pad_maximum_fusion), channel_id=1, replica_groups=mesh['mem'=16,'lat'=2] {'lat'}, dimensions={0} | all-to-all | bytes 33554432 | tf_op jit(solution)/shard_map/all_to_all | solution.py:33
  446.1 0.0 copy-start.2
  446.1 36.9 %copy.24 = bf16[4,64,2,128,128]{4,3,2,1,0:T(8,128)(2,1)} copy(bf16[4,64,2,128,128]{4,1,3,0,2:T(8,128)(2,1)S(1)} %bitcast.29) | data formatting | bytes 33554432 | tf_op jit(solution)/shard_map/reshape | solution.py:32
  483.0 0.0 copy-start.1
  483.0 0.0 copy-done.2
  483.0 12.0 %convolution_convert_fusion = bf16[4,64,128,256]{3,2,1,0:T(8,128)(2,1)} fusion(bf16[4,64,256,128]{3,2,1,0:T(8,128)(2,1)} %bitcast.30, bf16[256,256]{1,0:T(8,128)(2,1)S(1)} %copy-done.2), kind=kOutput, calls=%fused_computation.10 | convolution fusion | flops 4303355904 | bytes 33685504 | tf_op jit(solution)/shard_map/ac,mlcb->mlba/dot_general | solution.py:29
  494.9 0.0 copy-done.1
Async XLA Ops:
  6.5 216.8 %copy-start = (bf16[256,256]{1,0:T(8,128)(2,1)S(1)}, bf16[256,256]{1,0:T(8,128)(2,1)}, u32[]{:S(2)}) copy-start(bf16[256,256]{1,0:T(8,128)(2,1)} %param.12) | copy-start | bytes 393220
  6.5 17.8 %copy-start.5 = (f32[8,64]{1,0:T(8,128)S(1)}, f32[8,64]{1,0:T(8,128)}, u32[]{:S(2)}) copy-start(f32[8,64]{1,0:T(8,128)} %param.10) | copy-start | bytes 6148
  6.5 17.8 %copy-start.3 = (s32[128,256]{1,0:T(8,128)S(1)}, s32[128,256]{1,0:T(8,128)}, u32[]{:S(2)}) copy-start(s32[128,256]{1,0:T(8,128)} %param.9) | copy-start | bytes 393220
  6.5 124.1 %reduce-scatter.2.cloned.1.call-start = ((), (), s32[]{:S(2)}) async-start(), calls=%async_computation.2 | async-start | bytes 8912896 | tf_op jit(solution)/shard_map/reduce_scatter | solution.py:15
  24.3 182.5 %all-gather.2.cloned.1.call-start = ((), (), s32[]{:S(2)}) async-start(), calls=%async_computation.3 | async-start | bytes 8912896 | tf_op jit(solution)/shard_map/all_gather | solution.py:21
  132.6 90.8 %copy-start.4 = (bf16[64,64]{1,0:T(8,128)(2,1)S(1)}, bf16[64,64]{1,0:T(8,128)(2,1)}, u32[]{:S(2)}) copy-start(bf16[64,64]{1,0:T(8,128)(2,1)} %param.11) | copy-start | bytes 24580
  446.1 36.9 %copy-start.2 = (bf16[256,256]{1,0:T(8,128)(2,1)S(1)}, bf16[256,256]{1,0:T(8,128)(2,1)}, u32[]{:S(2)}) copy-start(bf16[256,256]{1,0:T(8,128)(2,1)} %param.13) | copy-start | bytes 393220
  483.0 12.0 %copy-start.1 = (bf16[256,256]{1,0:T(8,128)(2,1)S(1)}, bf16[256,256]{1,0:T(8,128)(2,1)}, u32[]{:S(2)}) copy-start(bf16[256,256]{1,0:T(8,128)(2,1)} %param.12) | copy-start | bytes 393220
Sparse Core Ops, SparseCore 0:
  24.4 106.1 reduce-scatter.1
  132.8 73.9 all-gather.1
